TPU v7x, 32 devices: a whole 2x2x4 slice. The times are simulated.
32 devices in a mesh: parts: 2 (over y), row: 4 (over z), col: 4 (over x, core).
Axes of the slice: x: 2, y: 2, z: 4, core: 2. Of those that a mesh axis runs over, the one named last changes fastest.
Arguments:
- amplitudes: bfloat16 [8, 100, 512, 512], P('parts', 'col', 'row'), parts along dimension 0, may hold values from -12 to 12
- integrals: bfloat16 [200, 512, 512], P(('parts', 'col'), 'row'), parts along dimension 0, may hold values from -0.109375 to 0.109375
- occ_irrep: int32 [200], P('parts'), parts along dimension 0, may hold values from 0 to 7, as said below
- vir_irrep: int32 [1024], P('parts'), parts along dimension 0, may hold values from 0 to 7, as said below
- screen: int32 [200, 8], P('parts'), parts along dimension 0, may hold values 0 or 1
- occ_energy: float32 [200], P('parts'), parts along dimension 0, may hold values from -1 to -0.3
- vir_energy: float32 [1024], P('parts'), parts along dimension 0, may hold values from 0.1 to 1
Outputs:
- update: float32 [512, 8, 512], P('row', 'parts', 'col'), parts along dimension 1
There are 2 independent parts, one for each index of `parts`. A program takes and returns all parts, laid end to end along the dimension named above; each array names one. Nothing has to cross between parts.
Inputs may be any that keep to these rules, and one draw needn't show every extreme that they name: `occ_irrep`: the labels never fall from one orbital to the next; the first is 0 and the last is 7. `vir_irrep`: the labels never fall from one orbital to the next and every label from 0 to 7 occurs; exactly one label covers 256 virtual orbitals, every other label fewer.
All inputs are finite; a program needn't handle non-finite values.
Results may differ from a plain program's by a relative error of at most 0.0003.
Values may be sent and summed in bfloat16 or wider, within the bound.
A program may use at most 128 MiB of HBM per device.

v0:
```python
import jax
import jax.numpy as jnp
from jax import lax
from jax.sharding import PartitionSpec as P


def folded_integrals(integrals, occ_local, vir_local, vir_irrep, screen_rows, pair_label):
    half = vir_irrep.shape[0] // 2
    irrep_codes = jnp.arange(8, dtype=jnp.int32)
    screen_local = jnp.sum(
        screen_rows[:, None, :] * (vir_local[None, :, None] == irrep_codes).astype(jnp.int32),
        axis=2,
    )
    wanted = jnp.bitwise_xor(jnp.bitwise_xor(occ_local[:, None], vir_local[None, :]), pair_label)
    wanted = jnp.where(screen_local == 1, wanted, -1)[:, :, None]
    zeros = jnp.zeros((), integrals.dtype)
    low = jnp.where(wanted == vir_irrep[None, None, :half], integrals[:, :, :half], zeros)
    return jnp.where(wanted == vir_irrep[None, None, half:], integrals[:, :, half:], low)


def on_device(amplitudes, integrals, occ_irrep, vir_irrep, screen, occ_energy, vir_energy):
    row_count = lax.axis_size("row")
    column_count = lax.axis_size("col")
    row, col = (lax.axis_index("row"), lax.axis_index("col"))
    batch_size, occ_share, vir_share, vir_total = amplitudes.shape
    half = vir_total // 2
    vir_columns = vir_total // column_count
    occ_offset = col * occ_share
    occ_local = lax.dynamic_slice_in_dim(occ_irrep, occ_offset, occ_share)
    vir_local = lax.dynamic_slice_in_dim(vir_irrep, row * vir_share, vir_share)
    screen_rows = lax.dynamic_slice_in_dim(screen, occ_offset, occ_share, 0)
    pair_label = occ_irrep[batch_size]
    folded = folded_integrals(integrals, occ_local, vir_local, vir_irrep, screen_rows, pair_label)
    gathered = lax.all_gather(folded, "row", axis=1, tiled=True)
    shift = jnp.bitwise_xor(occ_irrep[:batch_size, None], occ_local[None, :])
    keep_amp = (
        jnp.bitwise_xor(shift[:, :, None], vir_local[None, None, :])[:, :, :, None]
        == vir_irrep[None, None, None, :]
    )
    amp_kept = jnp.where(keep_amp, amplitudes, jnp.zeros_like(amplitudes))
    partial = lax.dot_general(
        amp_kept, gathered, (((1, 3), (0, 1)), ((), ())), preferred_element_type=jnp.float32
    )
    if row_count == column_count and column_count == 4:
        piece = lax.psum_scatter(partial, "col", scatter_dimension=2, tiled=True)
        routes = []
        for flip in (0, 1):
            pairs = []
            for r in range(row_count):
                for q in range(column_count):
                    target = q // 2 + 2 * ((q + flip) % 2)
                    pairs.append((r * column_count + q, target * column_count + r))
            routes.append(lax.ppermute(piece, ("row", "col"), pairs))
        swap = row // 2 == 1
        first = jnp.where(swap, routes[1], routes[0])
        second = jnp.where(swap, routes[0], routes[1])
        cycle = jnp.concatenate([first, second], axis=2)
    else:
        whole = lax.all_gather(lax.psum(partial, "col"), "row", axis=1, tiled=True)
        cycle = lax.dynamic_slice_in_dim(whole, col * vir_columns, vir_columns, 1)
        cycle = lax.dynamic_slice_in_dim(cycle, row * vir_share % half, vir_share, 2)
    cycle = jnp.transpose(cycle, (2, 0, 1))
    col_irrep = lax.dynamic_slice_in_dim(vir_irrep, col * vir_columns, vir_columns)
    kept = (
        jnp.bitwise_xor(occ_irrep[:batch_size, None], pair_label ^ col_irrep[None, :])[None]
        == vir_local[:, None, None]
    )
    cycle = jnp.where(kept, cycle, 0.0)
    energy_cols = lax.dynamic_slice_in_dim(vir_energy, col * vir_columns, vir_columns)
    energy_rows = lax.dynamic_slice_in_dim(vir_energy, row * vir_share, vir_share)
    denominator = (
        occ_energy[:batch_size][None, :, None]
        + occ_energy[batch_size]
        - energy_cols[None, None, :]
        - energy_rows[:, None, None]
    )
    return cycle / denominator


def solution(mesh):
    in_specs = (
        P("parts", "col", "row", None),
        P(("parts", "col"), "row", None),
        P("parts"),
        P("parts"),
        P("parts", None),
        P("parts"),
        P("parts"),
    )
    out_specs = P("row", "parts", "col")
    return jax.shard_map(
        on_device, mesh=mesh, in_specs=in_specs, out_specs=out_specs, check_vma=False
    )
```

profile of v0, /device:TPU:2, one launch (start us, length us, event | category | flops | bytes accessed | tf_op | source)
XLA Modules:
  0.0 192.5 jit_solution(17666716235107848208)
XLA Ops:
  6.5 1.2 slice.26
  7.8 0.8 fusion.14
  8.5 1.5 dynamic-slice_xor_fusion
  10.0 0.7 dynamic_slice.20
  10.8 0.1 copy.12
  10.9 3.4 %fusion.12 = (bf16[25,128,256]{2,1,0:T(8,128)(2,1)}, bf16[25,128,256]{2,1,0:T(8,128)(2,1)S(1)}) fusion(bf16[25,128,512]{2,1,0:T(8,128)(2,1)} %param.8), kind=kLoop, calls=%fused_computation.26 | loop fusion | bytes 6553600 | tf_op jit(solution)/shard_map/slice | solution.py:17
  14.4 2.1 %copy.17 = bf16[25,128,256]{1,2,0:T(8,128)(2,1)S(1)} copy(bf16[25,128,256]{2,1,0:T(8,128)(2,1)S(1)} %get-tuple-element.6) | data formatting | bytes 3276800
  16.5 3.1 %copy.18 = bf16[25,128,256]{1,2,0:T(8,128)(2,1)S(1)} copy(bf16[25,128,256]{2,1,0:T(8,128)(2,1)} %get-tuple-element.5) | data formatting | bytes 3276800
  19.6 0.1 multiply_reduce_fusion
  19.7 0.7 xor_select_fusion
  20.4 2.1 %compare_select_fusion.3 = bf16[25,128,256]{1,2,0:T(8,128)(2,1)} fusion(bf16[25,128,256]{1,2,0:T(8,128)(2,1)S(1)} %copy.17, bf16[25,128,256]{1,2,0:T(8,128)(2,1)S(1)} %copy.18, s32[25,128]{1,0:T(8,128)S(1)} %xor_select_fusion, s32[256]{0:T(256)S(1)} %get-tuple-element.14, s32[256]{0:T(256)S(1)} %get-tuple-element.13), kind=kLoop, calls=%fused_computation.7 | loop fusion | flops 3276800 | bytes 4930048 | tf_op jit(solution)/shard_map/jit(_where)/select_n | solution.py:18
  22.6 0.1 broadcast_xor_fusion
  22.7 10.7 %compare_select_fusion.8 = bf16[4,25,128,512]{3,2,1,0:T(8,128)(2,1)} fusion(bf16[4,25,128,512]{3,2,1,0:T(8,128)(2,1)} %param.7, s32[512]{0:T(512)S(1)} %copy-done.1, s32[4,25,128]{2,1,0:T(8,128)S(1)} %broadcast_xor_fusion), kind=kLoop, calls=%fused_computation.clone.clone.clone.clone.1 | loop fusion | flops 13107200 | bytes 26267648 | tf_op jit(solution)/shard_map/dot_general | solution.py:41
  33.4 109.6 %all-gather.2.cloned.1.call-done = bf16[25,512,256]{1,2,0:T(8,128)(2,1)} async-done(((bf16[25,128,256]{1,2,0:T(8,128)(2,1)}), bf16[25,512,256]{1,2,0:T(8,128)(2,1)}) %all-gather.2.cloned.1.call-update) | async-done | bytes 6553616 | tf_op jit(solution)/shard_map/all_gather | solution.py:34
  143.0 9.2 %fusion.5 = f32[4,128,256]{1,2,0:T(8,128)} fusion(bf16[25,512,256]{1,2,0:T(8,128)(2,1)} %all-gather.2.cloned.1.call-done, bf16[4,25,128,512]{3,2,1,0:T(8,128)(2,1)} %compare_select_fusion.8), kind=kOutput, calls=%fused_computation.8 | convolution fusion | flops 3355443200 | bytes 20185088 | tf_op jit(solution)/shard_map/dot_general | solution.py:41
  152.3 0.6 slice.32
  153.0 0.6 slice_add_fusion
  153.7 17.4 %reduce-scatter.2.cloned.1.call-done = f32[4,128,64]{1,2,0:T(8,128)} async-done(((f32[4,128,256]{1,2,0:T(8,128)}), f32[4,128,64]{1,2,0:T(8,128)}) %reduce-scatter.2.cloned.1.call-update) | async-done | bytes 131088 | tf_op jit(solution)/shard_map/reduce_scatter | solution.py:45
  171.1 4.5 %collective-permute-start = (f32[4,128,64]{1,2,0:T(8,128)}, f32[4,128,64]{1,2,0:T(8,128)S(1)}, u32[]{:S(2)}, u32[]{:S(2)}) collective-permute-start(f32[4,128,64]{1,2,0:T(8,128)} %reduce-scatter.2.cloned.1.call-done), channel_id=1, source_target_pairs={{0,8},{1,0},{2,12},{3,4},{4,9},{5,1},{6,13},{7,5},{8,10},{9,2},{10... | collective-permute-start | bytes 393224 | tf_op jit(solution)/shard_map/ppermute | solution.py:53
  175.6 1.9 collective-permute-start.1
  177.6 1.5 collective-permute-done
  179.0 5.6 %collective-permute-done.1 = f32[4,128,64]{1,2,0:T(8,128)S(1)} collective-permute-done((f32[4,128,64]{1,2,0:T(8,128)}, f32[4,128,64]{1,2,0:T(8,128)S(1)}, u32[]{:S(2)}, u32[]{:S(2)}) %collective-permute-start.1) | collective-permute-done | bytes 131104 | tf_op jit(solution)/shard_map/ppermute | solution.py:53
  184.7 0.1 fusion.9
  184.8 0.9 copy.15
  (21 shorter events, 0.5 us)
Async XLA Ops:
  6.5 4.2 %copy-start = (s32[100,8]{0,1:T(8,128)S(1)}, s32[100,8]{0,1:T(8,128)}, u32[]{:S(2)}) copy-start(s32[100,8]{0,1:T(8,128)} %param.11) | copy-start | bytes 9604
  6.5 136.5 %all-gather.2.cloned.1.call-start = ((), (), s32[]{:S(2)}) async-start(), calls=%async_computation.1 | async-start | bytes 8192000 | tf_op jit(solution)/shard_map/all_gather | solution.py:34
  20.4 2.1 %copy-start.2 = (s32[100]{0:T(128)S(1)}, s32[100]{0:T(128)}, u32[]{:S(2)}) copy-start(s32[100]{0:T(128)} %param.9) | copy-start | bytes 1204
  20.4 2.3 %copy-start.1 = (s32[512]{0:T(512)S(1)}, s32[512]{0:T(512)}, u32[]{:S(2)}) copy-start(s32[512]{0:T(512)} %param.10) | copy-start | bytes 6148
  22.5 148.6 %reduce-scatter.2.cloned.1.call-start = ((), (), s32[]{:S(2)}) async-start(), calls=%async_computation.2 | async-start | bytes 655360 | tf_op jit(solution)/shard_map/reduce_scatter | solution.py:45
  33.4 118.8 %copy-start.4 = (f32[100]{0:T(128)S(1)}, f32[100]{0:T(128)}, u32[]{:S(2)}) copy-start(f32[100]{0:T(128)} %param.12) | copy-start | bytes 1204
  33.4 119.4 %copy-start.3 = (f32[512]{0:T(512)S(1)}, f32[512]{0:T(512)}, u32[]{:S(2)}) copy-start(f32[512]{0:T(512)} %param.13) | copy-start | bytes 6148
  171.1 7.9 %collective-permute-start = (f32[4,128,64]{1,2,0:T(8,128)}, f32[4,128,64]{1,2,0:T(8,128)S(1)}, u32[]{:S(2)}, u32[]{:S(2)}) collective-permute-start(f32[4,128,64]{1,2,0:T(8,128)} %reduce-scatter.2.cloned.1.call-done), channel_id=1, source_target_pairs={{0,8},{1,0},{2,12},{3,4},{4,9},{5,1},{6,13},{7,5},{8,10},{9,2},{10... | collective-permute-start | bytes 393224 | tf_op jit(solution)/shard_map/ppermute | solution.py:53
  175.6 9.0 %collective-permute-start.1 = (f32[4,128,64]{1,2,0:T(8,128)}, f32[4,128,64]{1,2,0:T(8,128)S(1)}, u32[]{:S(2)}, u32[]{:S(2)}) collective-permute-start(f32[4,128,64]{1,2,0:T(8,128)} %reduce-scatter.2.cloned.1.call-done), channel_id=1, source_target_pairs={{0,0},{1,8},{2,4},{3,12},{4,1},{5,9},{6,5},{7,13},{8,2},{9,10},{10... | collective-permute-start | bytes 393224 | tf_op jit(solution)/shard_map/ppermute | solution.py:53
Sparse Core Ops, SparseCore 0:
  22.6 120.3 all-gather.1
  152.4 18.6 reduce-scatter.1
where the time goes:
time: 193 us; the launch traced here: 192 us
  waiting for transfers between devices  134 us (69%)
  other arithmetic  16.1 us (8%)
  between operations  13.5 us (7%)
  local copies, waits for them, and re-layouts  13.1 us (7%)
  matrix products  9.22 us (5%)
  starting transfers between devices  6.42 us (3%)
    all_gather x1, waiting for transfers between devices, on_device(): gathered = lax.all_gather(folded, 'row', axis=1, tiled=True)  110 us
    reduce_scatter x1, waiting for transfers between devices, on_device(): piece = lax.psum_scatter(partial, 'col', scatter_dimension=2, tiled=True)  17.4 us
    dot_general x1, other arithmetic, on_device(): lax.dot_general(amp_kept, gathered, (((1, 3), (0, 1)), ((), ())), preferr...  10.7 us
    dot_general x1, matrix products, on_device(): lax.dot_general(amp_kept, gathered, (((1, 3), (0, 1)), ((), ())), preferr...  9.22 us
    ppermute x2, waiting for transfers between devices, on_device(): routes.append(lax.ppermute(piece, ('row', 'col'), pairs))  7.05 us
    ppermute x2, starting transfers between devices, on_device(): routes.append(lax.ppermute(piece, ('row', 'col'), pairs))  6.37 us
    unnamed x12, local copies, waits for them, and re-layouts  5.25 us
  transfers between devices with their start and end apart: 4, of which 4 were waited for; matrix products, arithmetic and copies ran while one was open for 6% of the time, Pallas kernels for 0%

commit v1 on v0

--- a/solution.py
+++ b/solution.py
@@ -31,7 +31,26 @@
     screen_rows = lax.dynamic_slice_in_dim(screen, occ_offset, occ_share, 0)
     pair_label = occ_irrep[batch_size]
     folded = folded_integrals(integrals, occ_local, vir_local, vir_irrep, screen_rows, pair_label)
-    gathered = lax.all_gather(folded, "row", axis=1, tiled=True)
+    frame_in = folded
+    answer = lax.axis_size("row")
+    w2 = lax.axis_index("row")
+    arr_out, odd, opened = (answer, w2, frame_in.shape[1])
+    gathered = lax.dynamic_update_slice_in_dim(
+        jnp.zeros(
+            [dev * arr_out if t == 1 else dev for t, dev in enumerate(frame_in.shape)],
+            frame_in.dtype,
+        ),
+        frame_in,
+        odd * opened,
+        axis=1,
+    )
+    for pp in range(1, arr_out):
+        frame_in = lax.ppermute(
+            frame_in, axis_name="row", perm=[(t, (t + 1) % arr_out) for t in range(arr_out)]
+        )
+        gathered = lax.dynamic_update_slice_in_dim(
+            gathered, frame_in, (odd - pp) % arr_out * opened, axis=1
+        )
     shift = jnp.bitwise_xor(occ_irrep[:batch_size, None], occ_local[None, :])
     keep_amp = (
         jnp.bitwise_xor(shift[:, :, None], vir_local[None, None, :])[:, :, :, None]

time: 193 us -> 184 us (0.953)
  waiting for transfers between devices: 134 us -> 116 us
  local copies, waits for them, and re-layouts: 13.1 us -> 20.1 us
    all_gather x1 -> x0, waiting for transfers between devices: 110 us -> none  [on_device(): gathered = lax.all_gather(folded, 'row', axis=1, tiled=True)]
    ppermute x0 -> x3, waiting for transfers between devices: none -> 91.5 us  [on_device(): lax.ppermute(frame_in, axis_name='row', perm=[(t, (t + 1) % arr_out) for...]
    ppermute x0 -> x3, local copies, waits for them, and re-layouts: none -> 8.34 us  [on_device(): lax.ppermute(frame_in, axis_name='row', perm=[(t, (t + 1) % arr_out) for...]
    unnamed x12, local copies, waits for them, and re-layouts: 5.25 us -> 0.03 us
    dynamic_update_slice x0 -> x4, local copies, waits for them, and re-layouts: none -> 4.45 us  [the longest x3 4.06 us: on_device(): lax.dynamic_update_slice_in_dim(gathered, frame_in, (odd - pp) % arr_out...]
    slice x1 -> x0, local copies, waits for them, and re-layouts: 3.42 us -> none  [folded_integrals(): integrals[:, :, :half]]
    select_n x0 -> x1, local copies, waits for them, and re-layouts: none -> 2.11 us  [folded_integrals(): jnp.where(wanted == vir_irrep[None, None, half:], integrals[:, :, half:],...]
  transfers between devices with their start and end apart: 4 -> 6, of which waited for: 4 -> 6; matrix products, arithmetic and copies ran while one was open for 6% -> 13% of each run, Pallas kernels for 0% -> 0%
where the time goes in v1:
time: 184 us; the launch traced here: 183 us
  waiting for transfers between devices  116 us (63%)
  local copies, waits for them, and re-layouts  20.1 us (11%)
  other arithmetic  16.4 us (9%)
  between operations  13.6 us (7%)
  matrix products  9.24 us (5%)
  starting transfers between devices  8.01 us (4%)
    ppermute x3, waiting for transfers between devices, on_device(): lax.ppermute(frame_in, axis_name='row', perm=[(t, (t + 1) % arr_out) for...  91.5 us
    reduce_scatter x1, waiting for transfers between devices, on_device(): piece = lax.psum_scatter(partial, 'col', scatter_dimension=2, tiled=True)  17.4 us
    dot_general x1, other arithmetic, on_device(): lax.dot_general(amp_kept, gathered, (((1, 3), (0, 1)), ((), ())), preferr...  10.6 us
    dot_general x1, matrix products, on_device(): lax.dot_general(amp_kept, gathered, (((1, 3), (0, 1)), ((), ())), preferr...  9.24 us
    ppermute x3, local copies, waits for them, and re-layouts, on_device(): lax.ppermute(frame_in, axis_name='row', perm=[(t, (t + 1) % arr_out) for...  8.34 us
    ppermute x2, waiting for transfers between devices, on_device(): routes.append(lax.ppermute(piece, ('row', 'col'), pairs))  7.07 us
    ppermute x2, starting transfers between devices, on_device(): routes.append(lax.ppermute(piece, ('row', 'col'), pairs))  6.38 us
    dynamic_update_slice x3, local copies, waits for them, and re-layouts, on_device(): lax.dynamic_update_slice_in_dim(gathered, frame_in, (odd - pp) % arr_out...  4.06 us
  transfers between devices with their start and end apart: 6, of which 6 were waited for; matrix products, arithmetic and copies ran while one was open for 13% of the time, Pallas kernels for 0%

profile of v1, /device:TPU:2, one launch (start us, length us, event | category | flops | bytes accessed | tf_op | source)
XLA Modules:
  0.0 183.4 jit_solution(9004910136406322872)
XLA Ops:
  6.5 1.2 slice.26
  7.8 0.8 fusion.13
  8.5 1.5 dynamic-slice_xor_fusion
  10.0 0.7 dynamic_slice.20
  11.8 2.4 %compare_select_fusion.3 = bf16[25,128,256]{2,1,0:T(8,128)(2,1)S(1)} fusion(bf16[25,128,512]{2,1,0:T(8,128)(2,1)} %param.8, s32[256]{0:T(256)S(1)} %get-tuple-element.12, s32[256]{0:T(256)S(1)} %get-tuple-element.11, s32[25,128]{1,0:T(8,128)S(1)} %xor_select_fusion), kind=kLoop, calls=%fused_computation.7 | loop fusion | flops 3276800 | bytes 4930048 | tf_op jit(solution)/shard_map/jit(_where)/select_n | solution.py:18
  14.2 1.6 collective-permute-start
  15.9 37.9 %collective-permute-done = bf16[25,128,256]{2,1,0:T(8,128)(2,1)} collective-permute-done((bf16[25,128,256]{2,1,0:T(8,128)(2,1)S(1)}, bf16[25,128,256]{2,1,0:T(8,128)(2,1)}, u32[]{:S(2)}, u32[]{:S(2)}) %collective-permute-start) | collective-permute-done | bytes 1638432 | tf_op jit(solution)/shard_map/ppermute | solution.py:48
  53.8 2.1 %copy.15 = bf16[25,128,256]{1,2,0:T(8,128)(2,1)S(1)} copy(bf16[25,128,256]{2,1,0:T(8,128)(2,1)S(1)} %compare_select_fusion.3) | data formatting | bytes 3276800 | tf_op jit(solution)/shard_map/jit(_where)/select_n | solution.py:18
  57.3 35.4 %collective-permute-done.1 = bf16[25,128,256]{2,1,0:T(8,128)(2,1)} collective-permute-done((bf16[25,128,256]{2,1,0:T(8,128)(2,1)}, bf16[25,128,256]{2,1,0:T(8,128)(2,1)}, u32[]{:S(2)}, u32[]{:S(2)}) %collective-permute-start.1) | collective-permute-done | bytes 1638432 | tf_op jit(solution)/shard_map/ppermute | solution.py:48
  92.6 10.6 %compare_select_fusion.8 = bf16[4,25,128,512]{3,2,1,0:T(8,128)(2,1)} fusion(bf16[4,25,128,512]{3,2,1,0:T(8,128)(2,1)} %param.7, s32[512]{0:T(512)S(1)} %copy-done.2, s32[4,25,128]{2,1,0:T(8,128)S(1)} %broadcast_xor_fusion), kind=kLoop, calls=%fused_computation.clone.clone.clone.clone.1 | loop fusion | flops 13107200 | bytes 26267648 | tf_op jit(solution)/shard_map/dot_general | solution.py:60
  103.2 3.1 %copy.16 = bf16[25,128,256]{1,2,0:T(8,128)(2,1)S(1)} copy(bf16[25,128,256]{2,1,0:T(8,128)(2,1)} %collective-permute-done) | data formatting | bytes 3276800 | tf_op jit(solution)/shard_map/ppermute | solution.py:48
  106.4 1.4 constant_dynamic-update-slice_fusion.2
  107.8 3.1 %copy.17 = bf16[25,128,256]{1,2,0:T(8,128)(2,1)S(1)} copy(bf16[25,128,256]{2,1,0:T(8,128)(2,1)} %collective-permute-done.1) | data formatting | bytes 3276800 | tf_op jit(solution)/shard_map/ppermute | solution.py:48
  110.9 1.3 constant_dynamic-update-slice_fusion.1
  112.2 18.2 %collective-permute-done.2 = bf16[25,128,256]{2,1,0:T(8,128)(2,1)S(1)} collective-permute-done((bf16[25,128,256]{2,1,0:T(8,128)(2,1)}, bf16[25,128,256]{2,1,0:T(8,128)(2,1)S(1)}, u32[]{:S(2)}, u32[]{:S(2)}) %collective-permute-start.2) | collective-permute-done | bytes 1638432 | tf_op jit(solution)/shard_map/ppermute | solution.py:48
  130.5 2.1 %copy.18 = bf16[25,128,256]{1,2,0:T(8,128)(2,1)S(1)} copy(bf16[25,128,256]{2,1,0:T(8,128)(2,1)S(1)} %collective-permute-done.2) | data formatting | bytes 3276800 | tf_op jit(solution)/shard_map/ppermute | solution.py:48
  132.6 1.3 constant_dynamic-update-slice_fusion
  133.9 9.2 %fusion.5 = f32[4,128,256]{1,2,0:T(8,128)} fusion(bf16[25,512,256]{1,2,0:T(8,128)(2,1)} %constant_dynamic-update-slice_fusion, bf16[4,25,128,512]{3,2,1,0:T(8,128)(2,1)} %compare_select_fusion.8), kind=kOutput, calls=%fused_computation.8 | convolution fusion | flops 3355443200 | bytes 20185088 | tf_op jit(solution)/shard_map/dot_general | solution.py:60
  144.6 17.4 %reduce-scatter.2.cloned.1.call-done = f32[4,128,64]{1,2,0:T(8,128)} async-done(((f32[4,128,256]{1,2,0:T(8,128)}), f32[4,128,64]{1,2,0:T(8,128)}) %reduce-scatter.2.cloned.1.call-update) | async-done | bytes 131088 | tf_op jit(solution)/shard_map/reduce_scatter | solution.py:64
  162.0 4.5 %collective-permute-start.3 = (f32[4,128,64]{1,2,0:T(8,128)}, f32[4,128,64]{1,2,0:T(8,128)S(1)}, u32[]{:S(2)}, u32[]{:S(2)}) collective-permute-start(f32[4,128,64]{1,2,0:T(8,128)} %reduce-scatter.2.cloned.1.call-done), channel_id=1, source_target_pairs={{0,8},{1,0},{2,12},{3,4},{4,9},{5,1},{6,13},{7,5},{8,10},{9,2},{10... | collective-permute-start | bytes 393224 | tf_op jit(solution)/shard_map/ppermute | solution.py:72
  166.5 1.9 %collective-permute-start.4 = (f32[4,128,64]{1,2,0:T(8,128)}, f32[4,128,64]{1,2,0:T(8,128)S(1)}, u32[]{:S(2)}, u32[]{:S(2)}) collective-permute-start(f32[4,128,64]{1,2,0:T(8,128)} %reduce-scatter.2.cloned.1.call-done), channel_id=1, source_target_pairs={{0,0},{1,8},{2,4},{3,12},{4,1},{5,9},{6,5},{7,13},{8,2},{9,10},{10... | collective-permute-start | bytes 393224 | tf_op jit(solution)/shard_map/ppermute | solution.py:72
  168.5 1.5 collective-permute-done.3
  169.9 5.6 %collective-permute-done.4 = f32[4,128,64]{1,2,0:T(8,128)S(1)} collective-permute-done((f32[4,128,64]{1,2,0:T(8,128)}, f32[4,128,64]{1,2,0:T(8,128)S(1)}, u32[]{:S(2)}, u32[]{:S(2)}) %collective-permute-start.4) | collective-permute-done | bytes 131104 | tf_op jit(solution)/shard_map/ppermute | solution.py:72
  175.7 0.9 copy.19
  (32 shorter events, 3.9 us)
Async XLA Ops:
  6.5 4.2 %copy-start = (s32[100,8]{0,1:T(8,128)S(1)}, s32[100,8]{0,1:T(8,128)}, u32[]{:S(2)}) copy-start(s32[100,8]{0,1:T(8,128)} %param.11) | copy-start | bytes 9604
  6.5 155.5 %reduce-scatter.2.cloned.1.call-start = ((), (), s32[]{:S(2)}) async-start(), calls=%async_computation.1 | async-start | bytes 655360 | tf_op jit(solution)/shard_map/reduce_scatter | solution.py:64
  14.2 42.9 %copy-start.3 = (s32[100]{0:T(128)S(1)}, s32[100]{0:T(128)}, u32[]{:S(2)}) copy-start(s32[100]{0:T(128)} %param.9) | copy-start | bytes 1204
  14.2 78.4 %copy-start.2 = (s32[512]{0:T(512)S(1)}, s32[512]{0:T(512)}, u32[]{:S(2)}) copy-start(s32[512]{0:T(512)} %param.10) | copy-start | bytes 6148
  14.2 39.6 %collective-permute-start = (bf16[25,128,256]{2,1,0:T(8,128)(2,1)S(1)}, bf16[25,128,256]{2,1,0:T(8,128)(2,1)}, u32[]{:S(2)}, u32[]{:S(2)}) collective-permute-start(bf16[25,128,256]{2,1,0:T(8,128)(2,1)S(1)} %compare_select_fusion.3), channel_id=1, source_target_pairs={{0,4},{4,8},{8,12},{12,0},{1,5},{5,9},{9,13},{13,1},{2,6},{6,10},{... | collective-permute-start | bytes 4915208 | tf_op jit(solution)/shard_map/ppermute | solution.py:48
  53.8 38.9 %collective-permute-start.1 = (bf16[25,128,256]{2,1,0:T(8,128)(2,1)}, bf16[25,128,256]{2,1,0:T(8,128)(2,1)}, u32[]{:S(2)}, u32[]{:S(2)}) collective-permute-start(bf16[25,128,256]{2,1,0:T(8,128)(2,1)} %collective-permute-done), channel_id=1, source_target_pairs={{0,4},{4,8},{8,12},{12,0},{1,5},{5,9},{9,13},{13,1},{2,6},{6,10},{... | collective-permute-start | bytes 4915208 | tf_op jit(solution)/shard_map/ppermute | solution.py:48
  57.1 35.5 %copy-start.1 = (bf16[25,512,256]{1,2,0:T(8,128)(2,1)}, bf16[25,512,256]{1,2,0:T(8,128)(2,1)S(1)}, u32[]{:S(2)}) copy-start(bf16[25,512,256]{1,2,0:T(8,128)(2,1)S(1)} %constant_dynamic-update-slice_fusion.3) | copy-start | bytes 19660804
  92.6 37.8 %collective-permute-start.2 = (bf16[25,128,256]{2,1,0:T(8,128)(2,1)}, bf16[25,128,256]{2,1,0:T(8,128)(2,1)S(1)}, u32[]{:S(2)}, u32[]{:S(2)}) collective-permute-start(bf16[25,128,256]{2,1,0:T(8,128)(2,1)} %collective-permute-done.1), channel_id=1, source_target_pairs={{0,4},{4,8},{8,12},{12,0},{1,5},{5,9},{9,13},{13,1},{2,6},{6,10},{... | collective-permute-start | bytes 4915208 | tf_op jit(solution)/shard_map/ppermute | solution.py:48
  133.9 9.3 %copy-start.5 = (f32[100]{0:T(128)S(1)}, f32[100]{0:T(128)}, u32[]{:S(2)}) copy-start(f32[100]{0:T(128)} %param.12) | copy-start | bytes 1204
  133.9 9.9 %copy-start.4 = (f32[512]{0:T(512)S(1)}, f32[512]{0:T(512)}, u32[]{:S(2)}) copy-start(f32[512]{0:T(512)} %param.13) | copy-start | bytes 6148
  162.0 7.9 %collective-permute-start.3 = (f32[4,128,64]{1,2,0:T(8,128)}, f32[4,128,64]{1,2,0:T(8,128)S(1)}, u32[]{:S(2)}, u32[]{:S(2)}) collective-permute-start(f32[4,128,64]{1,2,0:T(8,128)} %reduce-scatter.2.cloned.1.call-done), channel_id=1, source_target_pairs={{0,8},{1,0},{2,12},{3,4},{4,9},{5,1},{6,13},{7,5},{8,10},{9,2},{10... | collective-permute-start | bytes 393224 | tf_op jit(solution)/shard_map/ppermute | solution.py:72
  166.5 9.1 %collective-permute-start.4 = (f32[4,128,64]{1,2,0:T(8,128)}, f32[4,128,64]{1,2,0:T(8,128)S(1)}, u32[]{:S(2)}, u32[]{:S(2)}) collective-permute-start(f32[4,128,64]{1,2,0:T(8,128)} %reduce-scatter.2.cloned.1.call-done), channel_id=1, source_target_pairs={{0,0},{1,8},{2,4},{3,12},{4,1},{5,9},{6,5},{7,13},{8,2},{9,10},{10... | collective-permute-start | bytes 393224 | tf_op jit(solution)/shard_map/ppermute | solution.py:72
Sparse Core Ops, SparseCore 0:
  143.3 18.6 reduce-scatter.1
